TPU v7x, 32 devices: a whole 2x2x4 slice. The times are simulated.
32 devices in a mesh: gx: 4 (over y, core), gy: 8 (over z, x).
Axes of the slice: x: 2, y: 2, z: 4, core: 2. Of those that a mesh axis runs over, the one named last changes fastest.
Arguments:
- velocity: float32 [3, 32, 64, 128], P(None, 'gx', 'gy'), may hold values from -6 to 6
- viscosity: float32 [32, 64, 128], P('gx', 'gy'), may hold values from 0.02 to 0.16
- forcing: float32 [4, 3, 32, 64, 128], P(None, None, 'gx', 'gy'), may hold values from -6 to 6
- earlier: float32 [60, 3, 32, 64, 128], P(None, None, 'gx', 'gy'), may hold values from -12 to 12
Outputs:
- velocity_out: float32 [3, 32, 64, 128], P(None, 'gx', 'gy')
- basis: float32 [64, 3, 32, 64, 128], P(None, None, 'gx', 'gy')
- factor: float32 [64, 64], replicated
All inputs are finite; a program needn't handle non-finite values.
Results may differ from a plain program's by a relative error of at most 0.000068.
Values sent between devices are 32-bit elements; how exact they have to be, the bound alone decides.
No kernel may reach another device: no remote copies, remote signals or barrier semaphores. Data moves between devices by JAX's collectives and lax.ppermute only.
A program may use at most 64 MiB of HBM per device.

v0:
```python
import jax
import jax.numpy as jnp
from jax import lax
from jax.sharding import PartitionSpec as P


def padded_2(array, sides, width):
    for axis, dim in sides:
        count, length = (lax.axis_size(axis), array.shape[dim])
        up = [(i, (i + 1) % count) for i in range(count - 1)]
        down = [(j, i) for i, j in up]
        last = lax.slice_in_dim(array, length - width, length, axis=dim)
        initial = lax.slice_in_dim(array, 0, width, axis=dim)
        before = lax.ppermute(last, axis, up)
        after = lax.ppermute(initial, axis, down)
        array = jnp.concatenate([before, array, after], axis=dim)
    return array


def laplace(padded, visc_pad):
    size_x = padded.shape[1] - 2
    size_y = padded.shape[2] - 2
    size_z = padded.shape[3] - 2
    centre = padded[:, 1 : 1 + size_x, 1 : 1 + size_y, 1 : 1 + size_z]
    visc_mid = visc_pad[1 : 1 + size_x, 1 : 1 + size_y, 1 : 1 + size_z]
    result = jnp.zeros_like(centre)
    for offset in ((2, 1, 1), (0, 1, 1), (1, 2, 1), (1, 0, 1), (1, 1, 2), (1, 1, 0)):
        first, second, third = offset
        beside = padded[:, first : first + size_x, second : second + size_y, third : third + size_z]
        visc_beside = visc_pad[
            first : first + size_x, second : second + size_y, third : third + size_z
        ]
        result = result + 0.5 * (visc_mid + visc_beside) * (beside - centre)
    return result


def factorize(panel, total_rows):
    local_gram = (
        lax.dot_general(
            panel,
            panel,
            (((1,), (1,)), ((), ())),
            precision=lax.Precision.HIGHEST,
            preferred_element_type=jnp.float32,
        )
        / total_rows
    )
    lower_factor = jnp.linalg.cholesky(lax.psum(local_gram, ("gx", "gy")))
    basis = jax.scipy.linalg.solve_triangular(lower_factor, panel, lower=True)
    return (lower_factor, basis)


def fields_rim_each(velocity, viscosity, forcing):
    visc_halo = padded_2(viscosity, (("gx", 0), ("gy", 1)), 1)
    visc_pad = jnp.pad(visc_halo, ((0, 0), (0, 0), (1, 1)))
    field = velocity
    fields = []
    for index in range(forcing.shape[0]):
        field_halo = padded_2(field, (("gx", 1), ("gy", 2)), 1)
        padded = jnp.pad(field_halo, ((0, 0), (0, 0), (0, 0), (1, 1)))
        field = field + laplace(padded, visc_pad) + forcing[index]
        fields.append(field)
    return fields


def local(velocity, viscosity, forcing, earlier):
    cell_rows = velocity.shape[0] * velocity.shape[1] * velocity.shape[2] * velocity.shape[3]
    total_rows = cell_rows * lax.axis_size("gx") * lax.axis_size("gy")
    fields = fields_rim_each(velocity, viscosity, forcing)
    panel_old = earlier.reshape(earlier.shape[0], cell_rows)
    snapshots = [field.reshape(1, cell_rows) for field in fields]
    lower_factor, basis = factorize(jnp.concatenate([panel_old] + snapshots, 0), total_rows)
    return (fields[-1], basis.reshape((basis.shape[0],) + velocity.shape), lower_factor.T)


def solution(mesh):
    return jax.shard_map(
        local,
        mesh=mesh,
        in_specs=(
            P(None, "gx", "gy", None),
            P("gx", "gy", None),
            P(None, None, "gx", "gy", None),
            P(None, None, "gx", "gy", None),
        ),
        out_specs=(P(None, "gx", "gy", None), P(None, None, "gx", "gy", None), P()),
        check_vma=False,
    )
```

profile of v0, /device:TPU:0, one launch (start us, length us, event | category | flops | bytes accessed | tf_op | source)
XLA Modules:
  0.0 195.6 jit_solution(2520877468651563737)
XLA Ops:
  0.6 0.9 fusion.91
  1.5 2.6 %collective-permute-start.2 = (f32[1,8,128]{2,1,0:T(8,128)S(1)}, f32[1,8,128]{2,1,0:T(8,128)S(1)}, u32[]{:S(2)}, u32[]{:S(2)}) collective-permute-start(f32[1,8,128]{2,1,0:T(8,128)S(1)} %get-tuple-element.39), channel_id=1, source_target_pairs={{0,8},{8,16},{16,24},{1,9},{9,17},{17,25},{2,10},{10,18},{18,26},{... | collective-permute-start | bytes 12296 | tf_op jit(solution)/shard_map/ppermute | solution.py:14
  4.1 1.3 collective-permute-start
  5.4 3.9 %collective-permute-done = f32[1,8,128]{2,1,0:T(8,128)S(1)} collective-permute-done((f32[1,8,128]{2,1,0:T(8,128)S(1)}, f32[1,8,128]{2,1,0:T(8,128)S(1)}, u32[]{:S(2)}, u32[]{:S(2)}) %collective-permute-start) | collective-permute-done | bytes 4128 | tf_op jit(solution)/shard_map/ppermute | solution.py:15
  9.3 0.9 fusion.81
  10.2 3.4 %collective-permute-start.6 = (f32[10,1,128]{2,1,0:T(1,128)S(1)}, f32[10,1,128]{2,1,0:T(1,128)S(1)}, u32[]{:S(2)}, u32[]{:S(2)}) collective-permute-start(f32[10,1,128]{2,1,0:T(1,128)S(1)} %get-tuple-element.29), channel_id=1, source_target_pairs={{0,1},{1,2},{2,3},{3,4},{4,5},{5,6},{6,7},{8,9},{9,10},{10,11},{11... | collective-permute-start | bytes 15368 | tf_op jit(solution)/shard_map/ppermute | solution.py:14
  13.6 1.3 collective-permute-start.4
  14.9 0.7 fusion.89
  15.6 1.3 collective-permute-start.1
  16.9 4.6 %collective-permute-start.3 = (f32[3,1,8,128]{3,2,1,0:T(8,128)S(1)}, f32[3,1,8,128]{3,2,1,0:T(8,128)S(1)}, u32[]{:S(2)}, u32[]{:S(2)}) collective-permute-start(f32[3,1,8,128]{3,2,1,0:T(8,128)S(1)} %get-tuple-element.26), channel_id=1, source_target_pairs={{0,8},{8,16},{16,24},{1,9},{9,17},{17,25},{2,10},{10,18},{18,26},{... | collective-permute-start | bytes 36872 | tf_op jit(solution)/shard_map/ppermute | solution.py:14
  22.4 0.9 constant_dynamic-update-slice_fusion.4
  23.3 4.3 %collective-permute-start.7 = (f32[3,10,1,128]{3,2,1,0:T(1,128)S(1)}, f32[3,10,1,128]{3,2,1,0:T(1,128)S(1)}, u32[]{:S(2)}, u32[]{:S(2)}) collective-permute-start(f32[3,10,1,128]{3,2,1,0:T(1,128)S(1)} %get-tuple-element.17), channel_id=1, source_target_pairs={{0,1},{1,2},{2,3},{3,4},{4,5},{5,6},{6,7},{8,9},{9,10},{10,11},{11... | collective-permute-start | bytes 46088 | tf_op jit(solution)/shard_map/ppermute | solution.py:14
  27.6 1.3 collective-permute-start.5
  28.9 0.8 fusion.77
  29.8 3.9 %collective-permute-done.5 = f32[3,10,1,128]{3,2,1,0:T(1,128)S(1)} collective-permute-done((f32[3,10,1,128]{3,2,1,0:T(1,128)S(1)}, f32[3,10,1,128]{3,2,1,0:T(1,128)S(1)}, u32[]{:S(2)}, u32[]{:S(2)}) %collective-permute-start.5) | collective-permute-done | bytes 15392 | tf_op jit(solution)/shard_map/ppermute | solution.py:15
  34.0 1.2 fusion.58
  35.2 2.5 %collective-permute-start.9 = (f32[3,1,8,128]{3,2,1,0:T(8,128)S(1)}, f32[3,1,8,128]{3,2,1,0:T(8,128)S(1)}, u32[]{:S(2)}, u32[]{:S(2)}) collective-permute-start(f32[3,1,8,128]{3,2,1,0:T(8,128)S(1)} %get-tuple-element.23), channel_id=1, source_target_pairs={{0,8},{8,16},{16,24},{1,9},{9,17},{17,25},{2,10},{10,18},{18,26},{... | collective-permute-start | bytes 36872 | tf_op jit(solution)/shard_map/ppermute | solution.py:14
  37.7 1.3 collective-permute-start.8
  39.0 4.7 %collective-permute-done.8 = f32[3,1,8,128]{3,2,1,0:T(8,128)S(1)} collective-permute-done((f32[3,1,8,128]{3,2,1,0:T(8,128)S(1)}, f32[3,1,8,128]{3,2,1,0:T(8,128)S(1)}, u32[]{:S(2)}, u32[]{:S(2)}) %collective-permute-start.8) | collective-permute-done | bytes 12320 | tf_op jit(solution)/shard_map/ppermute | solution.py:15
  43.7 4.8 %collective-permute-start.11 = (f32[3,10,1,128]{3,2,1,0:T(1,128)S(1)}, f32[3,10,1,128]{3,2,1,0:T(1,128)S(1)}, u32[]{:S(2)}, u32[]{:S(2)}) collective-permute-start(f32[3,10,1,128]{3,2,1,0:T(1,128)S(1)} %get-tuple-element.15), channel_id=1, source_target_pairs={{0,1},{1,2},{2,3},{3,4},{4,5},{5,6},{6,7},{8,9},{9,10},{10,11},{11... | collective-permute-start | bytes 46088 | tf_op jit(solution)/shard_map/ppermute | solution.py:14
  48.6 1.3 collective-permute-start.10
  50.0 4.2 %collective-permute-done.10 = f32[3,10,1,128]{3,2,1,0:T(1,128)S(1)} collective-permute-done((f32[3,10,1,128]{3,2,1,0:T(1,128)S(1)}, f32[3,10,1,128]{3,2,1,0:T(1,128)S(1)}, u32[]{:S(2)}, u32[]{:S(2)}) %collective-permute-start.10) | collective-permute-done | bytes 15392 | tf_op jit(solution)/shard_map/ppermute | solution.py:15
  54.5 1.0 fusion.41
  55.6 2.9 %collective-permute-start.13 = (f32[3,1,8,128]{3,2,1,0:T(8,128)S(1)}, f32[3,1,8,128]{3,2,1,0:T(8,128)S(1)}, u32[]{:S(2)}, u32[]{:S(2)}) collective-permute-start(f32[3,1,8,128]{3,2,1,0:T(8,128)S(1)} %get-tuple-element.21), channel_id=1, source_target_pairs={{0,8},{8,16},{16,24},{1,9},{9,17},{17,25},{2,10},{10,18},{18,26},{... | collective-permute-start | bytes 36872 | tf_op jit(solution)/shard_map/ppermute | solution.py:14
  58.5 1.3 collective-permute-start.12
  59.8 2.7 %collective-permute-done.12 = f32[3,1,8,128]{3,2,1,0:T(8,128)S(1)} collective-permute-done((f32[3,1,8,128]{3,2,1,0:T(8,128)S(1)}, f32[3,1,8,128]{3,2,1,0:T(8,128)S(1)}, u32[]{:S(2)}, u32[]{:S(2)}) %collective-permute-start.12) | collective-permute-done | bytes 12320 | tf_op jit(solution)/shard_map/ppermute | solution.py:15
  62.5 2.9 %collective-permute-start.15 = (f32[3,10,1,128]{3,2,1,0:T(1,128)S(1)}, f32[3,10,1,128]{3,2,1,0:T(1,128)S(1)}, u32[]{:S(2)}, u32[]{:S(2)}) collective-permute-start(f32[3,10,1,128]{3,2,1,0:T(1,128)S(1)} %get-tuple-element.13), channel_id=1, source_target_pairs={{0,1},{1,2},{2,3},{3,4},{4,5},{5,6},{6,7},{8,9},{9,10},{10,11},{11... | collective-permute-start | bytes 46088 | tf_op jit(solution)/shard_map/ppermute | solution.py:14
  65.5 1.3 collective-permute-start.14
  66.9 4.2 %collective-permute-done.14 = f32[3,10,1,128]{3,2,1,0:T(1,128)S(1)} collective-permute-done((f32[3,10,1,128]{3,2,1,0:T(1,128)S(1)}, f32[3,10,1,128]{3,2,1,0:T(1,128)S(1)}, u32[]{:S(2)}, u32[]{:S(2)}) %collective-permute-start.14) | collective-permute-done | bytes 15392 | tf_op jit(solution)/shard_map/ppermute | solution.py:15
  71.5 1.0 fusion.24
  72.5 3.2 %collective-permute-start.17 = (f32[3,1,8,128]{3,2,1,0:T(8,128)S(1)}, f32[3,1,8,128]{3,2,1,0:T(8,128)S(1)}, u32[]{:S(2)}, u32[]{:S(2)}) collective-permute-start(f32[3,1,8,128]{3,2,1,0:T(8,128)S(1)} %get-tuple-element.19), channel_id=1, source_target_pairs={{0,8},{8,16},{16,24},{1,9},{9,17},{17,25},{2,10},{10,18},{18,26},{... | collective-permute-start | bytes 36872 | tf_op jit(solution)/shard_map/ppermute | solution.py:14
  75.7 1.3 collective-permute-start.16
  77.0 2.4 %collective-permute-done.16 = f32[3,1,8,128]{3,2,1,0:T(8,128)S(1)} collective-permute-done((f32[3,1,8,128]{3,2,1,0:T(8,128)S(1)}, f32[3,1,8,128]{3,2,1,0:T(8,128)S(1)}, u32[]{:S(2)}, u32[]{:S(2)}) %collective-permute-start.16) | collective-permute-done | bytes 12320 | tf_op jit(solution)/shard_map/ppermute | solution.py:15
  79.5 4.8 %collective-permute-start.19 = (f32[3,10,1,128]{3,2,1,0:T(1,128)S(1)}, f32[3,10,1,128]{3,2,1,0:T(1,128)S(1)}, u32[]{:S(2)}, u32[]{:S(2)}) collective-permute-start(f32[3,10,1,128]{3,2,1,0:T(1,128)S(1)} %get-tuple-element.11), channel_id=1, source_target_pairs={{0,1},{1,2},{2,3},{3,4},{4,5},{5,6},{6,7},{8,9},{9,10},{10,11},{11... | collective-permute-start | bytes 46088 | tf_op jit(solution)/shard_map/ppermute | solution.py:14
  84.3 1.3 collective-permute-start.18
  85.6 1.0 pad.195
  86.6 6.3 %copy.21 = f32[8,8,192,128]{3,1,2,0:T(8,128)} copy(f32[8,8,192,128]{3,2,1,0:T(8,128)S(1)} %bitcast.40) | data formatting | bytes 12582912
  93.2 1.0 fusion.7
  94.3 17.8 %concatenate.123 = f32[64,24576]{1,0:T(8,128)} concatenate(f32[60,24576]{1,0:T(8,128)} %bitcast.38, f32[1,24576]{1,0:T(1,128)S(1)} %bitcast.42, f32[1,24576]{1,0:T(1,128)S(1)} %bitcast.43, f32[1,24576]{1,0:T(1,128)S(1)} %bitcast.44, f32[1,24576]{1,0:T(1,128)S(1)} %bitcast.45), dimensions={0} | concatenate | bytes 12582912 | tf_op jit(solution)/shard_map/concatenate | solution.py:72
  112.1 8.2 %convolution_multiply_fusion = f32[64,64]{0,1:T(8,128)S(1)} fusion(f32[64,24576]{1,0:T(8,128)} %concatenate.123), kind=kOutput, calls=%fused_computation.2 | convolution fusion | flops 1207963648 | bytes 6307840 | tf_op jit(solution)/shard_map/dot_general | solution.py:39
  120.2 42.6 %psum.7 = f32[64,64]{0,1:T(8,128)S(1)} all-reduce(f32[64,64]{0,1:T(8,128)S(1)} %convolution_multiply_fusion), channel_id=1, replica_groups=mesh['gx'=4,'gy'=8] {'gx','gy'}, use_global_device_ids=true, to_apply=%region_0.1 | all-reduce | flops 4096 | bytes 32768 | tf_op jit(solution)/shard_map/psum | solution.py:48
  163.0 5.8 %cholesky.16 = f32[64,64]{1,0:T(8,128)S(1)} custom-call(f32[64,64]{1,0:T(8,128)S(1)} %fusion.83), custom_call_target="Cholesky" | custom-call | tf_op jit(solution)/shard_map/jit(cholesky)/cholesky | solution.py:48
  169.5 0.7 fusion.84
  170.1 0.7 copy.17
  170.8 4.9 %custom-call.7 = f32[1,64,64]{1,2,0:T(8,128)S(1)} custom-call(f32[1,64,64]{2,1,0:T(8,128)S(1)} %get-tuple-element.32), custom_call_target="InvertDiagBlocksLowerTriangular" | custom-call | tf_op jit(solution)/shard_map/jit(_solve_triangular)/triangular_solve | solution.py:49
  175.7 3.9 %copy.22 = f32[8,8,192,128]{3,2,1,0:T(8,128)S(1)} copy(f32[8,8,192,128]{3,1,2,0:T(8,128)} %bitcast.37) | data formatting | bytes 12582912
  179.7 9.3 %fusion = f32[64,3,8,8,128]{4,0,3,2,1:T(8,128)S(1)} fusion(f32[3,8,8,128,64]{3,2,1,0,4:T(8,128)S(1)} %bitcast.39, f32[1,64,64]{1,2,0:T(8,128)S(1)} %custom-call.7), kind=kOutput, calls=%fused_computation | convolution fusion | flops 1207959552 | bytes 12599296 | tf_op jit(solution)/shard_map/jit(_solve_triangular)/triangular_solve | solution.py:49
  189.0 6.6 %copy.16 = f32[64,3,8,8,128]{4,3,2,1,0:T(8,128)} copy(f32[64,3,8,8,128]{4,0,3,2,1:T(8,128)S(1)} %fusion) | data formatting | bytes 12582912
  (38 shorter events, 3.3 us)
Async XLA Ops:
  0.6 85.0 %copy-start = (f32[60,3,8,8,128]{4,3,2,1,0:T(8,128)S(1)}, f32[60,3,8,8,128]{4,3,2,1,0:T(8,128)}, u32[]{:S(2)}) copy-start(f32[60,3,8,8,128]{4,3,2,1,0:T(8,128)} %param.7) | copy-start | bytes 17694724
  1.5 3.9 %collective-permute-start.2 = (f32[1,8,128]{2,1,0:T(8,128)S(1)}, f32[1,8,128]{2,1,0:T(8,128)S(1)}, u32[]{:S(2)}, u32[]{:S(2)}) collective-permute-start(f32[1,8,128]{2,1,0:T(8,128)S(1)} %get-tuple-element.39), channel_id=1, source_target_pairs={{0,8},{8,16},{16,24},{1,9},{9,17},{17,25},{2,10},{10,18},{18,26},{... | collective-permute-start | bytes 12296 | tf_op jit(solution)/shard_map/ppermute | solution.py:14
  4.1 5.2 %collective-permute-start = (f32[1,8,128]{2,1,0:T(8,128)S(1)}, f32[1,8,128]{2,1,0:T(8,128)S(1)}, u32[]{:S(2)}, u32[]{:S(2)}) collective-permute-start(f32[1,8,128]{2,1,0:T(8,128)S(1)} %get-tuple-element.38), channel_id=1, source_target_pairs={{8,0},{16,8},{24,16},{9,1},{17,9},{25,17},{10,2},{18,10},{26,18},{... | collective-permute-start | bytes 12296 | tf_op jit(solution)/shard_map/ppermute | solution.py:15
  10.2 11.3 %collective-permute-start.6 = (f32[10,1,128]{2,1,0:T(1,128)S(1)}, f32[10,1,128]{2,1,0:T(1,128)S(1)}, u32[]{:S(2)}, u32[]{:S(2)}) collective-permute-start(f32[10,1,128]{2,1,0:T(1,128)S(1)} %get-tuple-element.29), channel_id=1, source_target_pairs={{0,1},{1,2},{2,3},{3,4},{4,5},{5,6},{6,7},{8,9},{9,10},{10,11},{11... | collective-permute-start | bytes 15368 | tf_op jit(solution)/shard_map/ppermute | solution.py:14
  13.6 8.0 %collective-permute-start.4 = (f32[10,1,128]{2,1,0:T(1,128)S(1)}, f32[10,1,128]{2,1,0:T(1,128)S(1)}, u32[]{:S(2)}, u32[]{:S(2)}) collective-permute-start(f32[10,1,128]{2,1,0:T(1,128)S(1)} %get-tuple-element.30), channel_id=1, source_target_pairs={{1,0},{2,1},{3,2},{4,3},{5,4},{6,5},{7,6},{9,8},{10,9},{11,10},{12... | collective-permute-start | bytes 15368 | tf_op jit(solution)/shard_map/ppermute | solution.py:15
  15.6 7.6 %collective-permute-start.1 = (f32[3,1,8,128]{3,2,1,0:T(8,128)S(1)}, f32[3,1,8,128]{3,2,1,0:T(8,128)S(1)}, u32[]{:S(2)}, u32[]{:S(2)}) collective-permute-start(f32[3,1,8,128]{3,2,1,0:T(8,128)S(1)} %get-tuple-element.25), channel_id=1, source_target_pairs={{8,0},{16,8},{24,16},{9,1},{17,9},{25,17},{10,2},{18,10},{26,18},{... | collective-permute-start | bytes 36872 | tf_op jit(solution)/shard_map/ppermute | solution.py:15
  16.9 5.4 %collective-permute-start.3 = (f32[3,1,8,128]{3,2,1,0:T(8,128)S(1)}, f32[3,1,8,128]{3,2,1,0:T(8,128)S(1)}, u32[]{:S(2)}, u32[]{:S(2)}) collective-permute-start(f32[3,1,8,128]{3,2,1,0:T(8,128)S(1)} %get-tuple-element.26), channel_id=1, source_target_pairs={{0,8},{8,16},{16,24},{1,9},{9,17},{17,25},{2,10},{10,18},{18,26},{... | collective-permute-start | bytes 36872 | tf_op jit(solution)/shard_map/ppermute | solution.py:14
  23.3 6.4 %collective-permute-start.7 = (f32[3,10,1,128]{3,2,1,0:T(1,128)S(1)}, f32[3,10,1,128]{3,2,1,0:T(1,128)S(1)}, u32[]{:S(2)}, u32[]{:S(2)}) collective-permute-start(f32[3,10,1,128]{3,2,1,0:T(1,128)S(1)} %get-tuple-element.17), channel_id=1, source_target_pairs={{0,1},{1,2},{2,3},{3,4},{4,5},{5,6},{6,7},{8,9},{9,10},{10,11},{11... | collective-permute-start | bytes 46088 | tf_op jit(solution)/shard_map/ppermute | solution.py:14
  27.6 6.1 %collective-permute-start.5 = (f32[3,10,1,128]{3,2,1,0:T(1,128)S(1)}, f32[3,10,1,128]{3,2,1,0:T(1,128)S(1)}, u32[]{:S(2)}, u32[]{:S(2)}) collective-permute-start(f32[3,10,1,128]{3,2,1,0:T(1,128)S(1)} %get-tuple-element.18), channel_id=1, source_target_pairs={{1,0},{2,1},{3,2},{4,3},{5,4},{6,5},{7,6},{9,8},{10,9},{11,10},{12... | collective-permute-start | bytes 46088 | tf_op jit(solution)/shard_map/ppermute | solution.py:15
  35.2 3.8 %collective-permute-start.9 = (f32[3,1,8,128]{3,2,1,0:T(8,128)S(1)}, f32[3,1,8,128]{3,2,1,0:T(8,128)S(1)}, u32[]{:S(2)}, u32[]{:S(2)}) collective-permute-start(f32[3,1,8,128]{3,2,1,0:T(8,128)S(1)} %get-tuple-element.23), channel_id=1, source_target_pairs={{0,8},{8,16},{16,24},{1,9},{9,17},{17,25},{2,10},{10,18},{18,26},{... | collective-permute-start | bytes 36872 | tf_op jit(solution)/shard_map/ppermute | solution.py:14
  37.7 6.0 %collective-permute-start.8 = (f32[3,1,8,128]{3,2,1,0:T(8,128)S(1)}, f32[3,1,8,128]{3,2,1,0:T(8,128)S(1)}, u32[]{:S(2)}, u32[]{:S(2)}) collective-permute-start(f32[3,1,8,128]{3,2,1,0:T(8,128)S(1)} %get-tuple-element.24), channel_id=1, source_target_pairs={{8,0},{16,8},{24,16},{9,1},{17,9},{25,17},{10,2},{18,10},{26,18},{... | collective-permute-start | bytes 36872 | tf_op jit(solution)/shard_map/ppermute | solution.py:15
  43.7 6.2 %collective-permute-start.11 = (f32[3,10,1,128]{3,2,1,0:T(1,128)S(1)}, f32[3,10,1,128]{3,2,1,0:T(1,128)S(1)}, u32[]{:S(2)}, u32[]{:S(2)}) collective-permute-start(f32[3,10,1,128]{3,2,1,0:T(1,128)S(1)} %get-tuple-element.15), channel_id=1, source_target_pairs={{0,1},{1,2},{2,3},{3,4},{4,5},{5,6},{6,7},{8,9},{9,10},{10,11},{11... | collective-permute-start | bytes 46088 | tf_op jit(solution)/shard_map/ppermute | solution.py:14
  48.6 5.6 %collective-permute-start.10 = (f32[3,10,1,128]{3,2,1,0:T(1,128)S(1)}, f32[3,10,1,128]{3,2,1,0:T(1,128)S(1)}, u32[]{:S(2)}, u32[]{:S(2)}) collective-permute-start(f32[3,10,1,128]{3,2,1,0:T(1,128)S(1)} %get-tuple-element.16), channel_id=1, source_target_pairs={{1,0},{2,1},{3,2},{4,3},{5,4},{6,5},{7,6},{9,8},{10,9},{11,10},{12... | collective-permute-start | bytes 46088 | tf_op jit(solution)/shard_map/ppermute | solution.py:15
  55.6 4.2 %collective-permute-start.13 = (f32[3,1,8,128]{3,2,1,0:T(8,128)S(1)}, f32[3,1,8,128]{3,2,1,0:T(8,128)S(1)}, u32[]{:S(2)}, u32[]{:S(2)}) collective-permute-start(f32[3,1,8,128]{3,2,1,0:T(8,128)S(1)} %get-tuple-element.21), channel_id=1, source_target_pairs={{0,8},{8,16},{16,24},{1,9},{9,17},{17,25},{2,10},{10,18},{18,26},{... | collective-permute-start | bytes 36872 | tf_op jit(solution)/shard_map/ppermute | solution.py:14
  58.5 4.0 %collective-permute-start.12 = (f32[3,1,8,128]{3,2,1,0:T(8,128)S(1)}, f32[3,1,8,128]{3,2,1,0:T(8,128)S(1)}, u32[]{:S(2)}, u32[]{:S(2)}) collective-permute-start(f32[3,1,8,128]{3,2,1,0:T(8,128)S(1)} %get-tuple-element.22), channel_id=1, source_target_pairs={{8,0},{16,8},{24,16},{9,1},{17,9},{25,17},{10,2},{18,10},{26,18},{... | collective-permute-start | bytes 36872 | tf_op jit(solution)/shard_map/ppermute | solution.py:15
  62.5 4.4 %collective-permute-start.15 = (f32[3,10,1,128]{3,2,1,0:T(1,128)S(1)}, f32[3,10,1,128]{3,2,1,0:T(1,128)S(1)}, u32[]{:S(2)}, u32[]{:S(2)}) collective-permute-start(f32[3,10,1,128]{3,2,1,0:T(1,128)S(1)} %get-tuple-element.13), channel_id=1, source_target_pairs={{0,1},{1,2},{2,3},{3,4},{4,5},{5,6},{6,7},{8,9},{9,10},{10,11},{11... | collective-permute-start | bytes 46088 | tf_op jit(solution)/shard_map/ppermute | solution.py:14
  65.5 5.6 %collective-permute-start.14 = (f32[3,10,1,128]{3,2,1,0:T(1,128)S(1)}, f32[3,10,1,128]{3,2,1,0:T(1,128)S(1)}, u32[]{:S(2)}, u32[]{:S(2)}) collective-permute-start(f32[3,10,1,128]{3,2,1,0:T(1,128)S(1)} %get-tuple-element.14), channel_id=1, source_target_pairs={{1,0},{2,1},{3,2},{4,3},{5,4},{6,5},{7,6},{9,8},{10,9},{11,10},{12... | collective-permute-start | bytes 46088 | tf_op jit(solution)/shard_map/ppermute | solution.py:15
  72.5 4.5 %collective-permute-start.17 = (f32[3,1,8,128]{3,2,1,0:T(8,128)S(1)}, f32[3,1,8,128]{3,2,1,0:T(8,128)S(1)}, u32[]{:S(2)}, u32[]{:S(2)}) collective-permute-start(f32[3,1,8,128]{3,2,1,0:T(8,128)S(1)} %get-tuple-element.19), channel_id=1, source_target_pairs={{0,8},{8,16},{16,24},{1,9},{9,17},{17,25},{2,10},{10,18},{18,26},{... | collective-permute-start | bytes 36872 | tf_op jit(solution)/shard_map/ppermute | solution.py:14
  75.7 3.8 %collective-permute-start.16 = (f32[3,1,8,128]{3,2,1,0:T(8,128)S(1)}, f32[3,1,8,128]{3,2,1,0:T(8,128)S(1)}, u32[]{:S(2)}, u32[]{:S(2)}) collective-permute-start(f32[3,1,8,128]{3,2,1,0:T(8,128)S(1)} %get-tuple-element.20), channel_id=1, source_target_pairs={{8,0},{16,8},{24,16},{9,1},{17,9},{25,17},{10,2},{18,10},{26,18},{... | collective-permute-start | bytes 36872 | tf_op jit(solution)/shard_map/ppermute | solution.py:15
  79.5 13.4 %collective-permute-start.19 = (f32[3,10,1,128]{3,2,1,0:T(1,128)S(1)}, f32[3,10,1,128]{3,2,1,0:T(1,128)S(1)}, u32[]{:S(2)}, u32[]{:S(2)}) collective-permute-start(f32[3,10,1,128]{3,2,1,0:T(1,128)S(1)} %get-tuple-element.11), channel_id=1, source_target_pairs={{0,1},{1,2},{2,3},{3,4},{4,5},{5,6},{6,7},{8,9},{9,10},{10,11},{11... | collective-permute-start | bytes 46088 | tf_op jit(solution)/shard_map/ppermute | solution.py:14
  84.3 8.6 %collective-permute-start.18 = (f32[3,10,1,128]{3,2,1,0:T(1,128)S(1)}, f32[3,10,1,128]{3,2,1,0:T(1,128)S(1)}, u32[]{:S(2)}, u32[]{:S(2)}) collective-permute-start(f32[3,10,1,128]{3,2,1,0:T(1,128)S(1)} %get-tuple-element.12), channel_id=1, source_target_pairs={{1,0},{2,1},{3,2},{4,3},{5,4},{6,5},{7,6},{9,8},{10,9},{11,10},{12... | collective-permute-start | bytes 46088 | tf_op jit(solution)/shard_map/ppermute | solution.py:15
  94.3 17.8 %copy-start.1 = (f32[3,8,8,128]{3,2,1,0:T(8,128)}, f32[3,8,8,128]{3,2,1,0:T(8,128)S(1)}, u32[]{:S(2)}) copy-start(f32[3,8,8,128]{3,2,1,0:T(8,128)S(1)} %fusion.7) | copy-start | bytes 294916
where the time goes:
time: 197 us; the launch traced here: 196 us
  starting transfers between devices  49 us (25%)
  blocking collectives  42.6 us (22%)
  local copies, waits for them, and re-layouts  38.9 us (20%)
  waiting for transfers between devices  27 us (14%)
  other arithmetic  19.6 us (10%)
  matrix products  17.5 us (9%)
    psum x1, blocking collectives, factorize(): lower_factor = jnp.linalg.cholesky(lax.psum(local_gram, ('gx', 'gy')))  42.6 us
    ppermute x10, starting transfers between devices, padded_2(): before = lax.ppermute(last, axis, up)  36.1 us
    ppermute x10, waiting for transfers between devices, padded_2(): after = lax.ppermute(initial, axis, down)  26.1 us
    unnamed x12, local copies, waits for them, and re-layouts  19.4 us
    concatenate x1, local copies, waits for them, and re-layouts, local(): jnp.concatenate([panel_old] + snapshots, 0)  17.8 us
    ppermute x10, starting transfers between devices, padded_2(): after = lax.ppermute(initial, axis, down)  12.9 us
    another operation x1, matrix products, factorize(): basis = jax.scipy.linalg.solve_triangular(lower_factor, panel, lower=True)  9.33 us
    dot_general x1, matrix products, factorize(): lax.dot_general(panel, panel, (((1,), (1,)), ((), ())), precision=lax.Pre...  8.18 us
  transfers between devices with their start and end apart: 20, of which 10 were waited for; matrix products, arithmetic and copies ran while one was open for 5% of the time, Pallas kernels for 0%

commit v1 on v0

--- a/solution.py
+++ b/solution.py
@@ -45,7 +45,7 @@
         )
         / total_rows
     )
-    lower_factor = jnp.linalg.cholesky(lax.psum(local_gram, ("gx", "gy")))
+    lower_factor = jnp.linalg.cholesky(lax.psum(lax.psum(local_gram, "gx"), "gy"))
     basis = jax.scipy.linalg.solve_triangular(lower_factor, panel, lower=True)
     return (lower_factor, basis)
 

time: 197 us -> 202 us (1.025)
  blocking collectives: 42.6 us -> 47.7 us
    psum x1 -> x2, blocking collectives: 42.6 us -> 47.7 us  [the longest x1 35.4 us: factorize(): lax.psum(lax.psum(local_gram, 'gx'), 'gy')]
where the time goes in v1:
time: 202 us; the launch traced here: 201 us
  starting transfers between devices  49 us (24%)
  blocking collectives  47.7 us (24%)
  local copies, waits for them, and re-layouts  38.8 us (19%)
  waiting for transfers between devices  27 us (13%)
  other arithmetic  19.6 us (10%)
  matrix products  17.5 us (9%)
    ppermute x10, starting transfers between devices, padded_2(): before = lax.ppermute(last, axis, up)  36.1 us
    psum x1, blocking collectives, factorize(): lax.psum(lax.psum(local_gram, 'gx'), 'gy')  35.4 us
    ppermute x10, waiting for transfers between devices, padded_2(): after = lax.ppermute(initial, axis, down)  26.1 us
    unnamed x12, local copies, waits for them, and re-layouts  19.4 us
    concatenate x1, local copies, waits for them, and re-layouts, local(): jnp.concatenate([panel_old] + snapshots, 0)  17.7 us
    ppermute x10, starting transfers between devices, padded_2(): after = lax.ppermute(initial, axis, down)  12.9 us
    psum x1, blocking collectives, factorize(): lax.psum(local_gram, 'gx')  12.3 us
    another operation x1, matrix products, factorize(): basis = jax.scipy.linalg.solve_triangular(lower_factor, panel, lower=True)  9.33 us
  transfers between devices with their start and end apart: 20, of which 10 were waited for; matrix products, arithmetic and copies ran while one was open for 5% of the time, Pallas kernels for 0%

profile of v1, /device:TPU:0, one launch (start us, length us, event | category | flops | bytes accessed | tf_op | source)
XLA Modules:
  0.0 200.6 jit_solution(14532236857107992846)
XLA Ops:
  0.6 0.9 fusion.91
  1.5 2.6 %collective-permute-start.2 = (f32[1,8,128]{2,1,0:T(8,128)S(1)}, f32[1,8,128]{2,1,0:T(8,128)S(1)}, u32[]{:S(2)}, u32[]{:S(2)}) collective-permute-start(f32[1,8,128]{2,1,0:T(8,128)S(1)} %get-tuple-element.39), channel_id=1, source_target_pairs={{0,8},{8,16},{16,24},{1,9},{9,17},{17,25},{2,10},{10,18},{18,26},{... | collective-permute-start | bytes 12296 | tf_op jit(solution)/shard_map/ppermute | solution.py:14
  4.1 1.3 collective-permute-start
  5.4 3.9 %collective-permute-done = f32[1,8,128]{2,1,0:T(8,128)S(1)} collective-permute-done((f32[1,8,128]{2,1,0:T(8,128)S(1)}, f32[1,8,128]{2,1,0:T(8,128)S(1)}, u32[]{:S(2)}, u32[]{:S(2)}) %collective-permute-start) | collective-permute-done | bytes 4128 | tf_op jit(solution)/shard_map/ppermute | solution.py:15
  9.3 0.9 fusion.81
  10.2 3.4 %collective-permute-start.6 = (f32[10,1,128]{2,1,0:T(1,128)S(1)}, f32[10,1,128]{2,1,0:T(1,128)S(1)}, u32[]{:S(2)}, u32[]{:S(2)}) collective-permute-start(f32[10,1,128]{2,1,0:T(1,128)S(1)} %get-tuple-element.29), channel_id=1, source_target_pairs={{0,1},{1,2},{2,3},{3,4},{4,5},{5,6},{6,7},{8,9},{9,10},{10,11},{11... | collective-permute-start | bytes 15368 | tf_op jit(solution)/shard_map/ppermute | solution.py:14
  13.6 1.3 collective-permute-start.4
  14.9 0.7 fusion.89
  15.6 1.3 collective-permute-start.1
  16.9 4.6 %collective-permute-start.3 = (f32[3,1,8,128]{3,2,1,0:T(8,128)S(1)}, f32[3,1,8,128]{3,2,1,0:T(8,128)S(1)}, u32[]{:S(2)}, u32[]{:S(2)}) collective-permute-start(f32[3,1,8,128]{3,2,1,0:T(8,128)S(1)} %get-tuple-element.26), channel_id=1, source_target_pairs={{0,8},{8,16},{16,24},{1,9},{9,17},{17,25},{2,10},{10,18},{18,26},{... | collective-permute-start | bytes 36872 | tf_op jit(solution)/shard_map/ppermute | solution.py:14
  22.4 0.9 constant_dynamic-update-slice_fusion.4
  23.3 4.3 %collective-permute-start.7 = (f32[3,10,1,128]{3,2,1,0:T(1,128)S(1)}, f32[3,10,1,128]{3,2,1,0:T(1,128)S(1)}, u32[]{:S(2)}, u32[]{:S(2)}) collective-permute-start(f32[3,10,1,128]{3,2,1,0:T(1,128)S(1)} %get-tuple-element.17), channel_id=1, source_target_pairs={{0,1},{1,2},{2,3},{3,4},{4,5},{5,6},{6,7},{8,9},{9,10},{10,11},{11... | collective-permute-start | bytes 46088 | tf_op jit(solution)/shard_map/ppermute | solution.py:14
  27.6 1.3 collective-permute-start.5
  28.9 0.8 fusion.77
  29.8 3.9 %collective-permute-done.5 = f32[3,10,1,128]{3,2,1,0:T(1,128)S(1)} collective-permute-done((f32[3,10,1,128]{3,2,1,0:T(1,128)S(1)}, f32[3,10,1,128]{3,2,1,0:T(1,128)S(1)}, u32[]{:S(2)}, u32[]{:S(2)}) %collective-permute-start.5) | collective-permute-done | bytes 15392 | tf_op jit(solution)/shard_map/ppermute | solution.py:15
  34.0 1.2 fusion.58
  35.2 2.5 %collective-permute-start.9 = (f32[3,1,8,128]{3,2,1,0:T(8,128)S(1)}, f32[3,1,8,128]{3,2,1,0:T(8,128)S(1)}, u32[]{:S(2)}, u32[]{:S(2)}) collective-permute-start(f32[3,1,8,128]{3,2,1,0:T(8,128)S(1)} %get-tuple-element.23), channel_id=1, source_target_pairs={{0,8},{8,16},{16,24},{1,9},{9,17},{17,25},{2,10},{10,18},{18,26},{... | collective-permute-start | bytes 36872 | tf_op jit(solution)/shard_map/ppermute | solution.py:14
  37.7 1.3 collective-permute-start.8
  39.0 4.7 %collective-permute-done.8 = f32[3,1,8,128]{3,2,1,0:T(8,128)S(1)} collective-permute-done((f32[3,1,8,128]{3,2,1,0:T(8,128)S(1)}, f32[3,1,8,128]{3,2,1,0:T(8,128)S(1)}, u32[]{:S(2)}, u32[]{:S(2)}) %collective-permute-start.8) | collective-permute-done | bytes 12320 | tf_op jit(solution)/shard_map/ppermute | solution.py:15
  43.7 4.8 %collective-permute-start.11 = (f32[3,10,1,128]{3,2,1,0:T(1,128)S(1)}, f32[3,10,1,128]{3,2,1,0:T(1,128)S(1)}, u32[]{:S(2)}, u32[]{:S(2)}) collective-permute-start(f32[3,10,1,128]{3,2,1,0:T(1,128)S(1)} %get-tuple-element.15), channel_id=1, source_target_pairs={{0,1},{1,2},{2,3},{3,4},{4,5},{5,6},{6,7},{8,9},{9,10},{10,11},{11... | collective-permute-start | bytes 46088 | tf_op jit(solution)/shard_map/ppermute | solution.py:14
  48.6 1.3 collective-permute-start.10
  50.0 4.2 %collective-permute-done.10 = f32[3,10,1,128]{3,2,1,0:T(1,128)S(1)} collective-permute-done((f32[3,10,1,128]{3,2,1,0:T(1,128)S(1)}, f32[3,10,1,128]{3,2,1,0:T(1,128)S(1)}, u32[]{:S(2)}, u32[]{:S(2)}) %collective-permute-start.10) | collective-permute-done | bytes 15392 | tf_op jit(solution)/shard_map/ppermute | solution.py:15
  54.5 1.0 fusion.41
  55.6 2.9 %collective-permute-start.13 = (f32[3,1,8,128]{3,2,1,0:T(8,128)S(1)}, f32[3,1,8,128]{3,2,1,0:T(8,128)S(1)}, u32[]{:S(2)}, u32[]{:S(2)}) collective-permute-start(f32[3,1,8,128]{3,2,1,0:T(8,128)S(1)} %get-tuple-element.21), channel_id=1, source_target_pairs={{0,8},{8,16},{16,24},{1,9},{9,17},{17,25},{2,10},{10,18},{18,26},{... | collective-permute-start | bytes 36872 | tf_op jit(solution)/shard_map/ppermute | solution.py:14
  58.5 1.3 collective-permute-start.12
  59.8 2.7 %collective-permute-done.12 = f32[3,1,8,128]{3,2,1,0:T(8,128)S(1)} collective-permute-done((f32[3,1,8,128]{3,2,1,0:T(8,128)S(1)}, f32[3,1,8,128]{3,2,1,0:T(8,128)S(1)}, u32[]{:S(2)}, u32[]{:S(2)}) %collective-permute-start.12) | collective-permute-done | bytes 12320 | tf_op jit(solution)/shard_map/ppermute | solution.py:15
  62.5 2.9 %collective-permute-start.15 = (f32[3,10,1,128]{3,2,1,0:T(1,128)S(1)}, f32[3,10,1,128]{3,2,1,0:T(1,128)S(1)}, u32[]{:S(2)}, u32[]{:S(2)}) collective-permute-start(f32[3,10,1,128]{3,2,1,0:T(1,128)S(1)} %get-tuple-element.13), channel_id=1, source_target_pairs={{0,1},{1,2},{2,3},{3,4},{4,5},{5,6},{6,7},{8,9},{9,10},{10,11},{11... | collective-permute-start | bytes 46088 | tf_op jit(solution)/shard_map/ppermute | solution.py:14
  65.5 1.3 collective-permute-start.14
  66.9 4.2 %collective-permute-done.14 = f32[3,10,1,128]{3,2,1,0:T(1,128)S(1)} collective-permute-done((f32[3,10,1,128]{3,2,1,0:T(1,128)S(1)}, f32[3,10,1,128]{3,2,1,0:T(1,128)S(1)}, u32[]{:S(2)}, u32[]{:S(2)}) %collective-permute-start.14) | collective-permute-done | bytes 15392 | tf_op jit(solution)/shard_map/ppermute | solution.py:15
  71.5 1.0 fusion.24
  72.5 3.2 %collective-permute-start.17 = (f32[3,1,8,128]{3,2,1,0:T(8,128)S(1)}, f32[3,1,8,128]{3,2,1,0:T(8,128)S(1)}, u32[]{:S(2)}, u32[]{:S(2)}) collective-permute-start(f32[3,1,8,128]{3,2,1,0:T(8,128)S(1)} %get-tuple-element.19), channel_id=1, source_target_pairs={{0,8},{8,16},{16,24},{1,9},{9,17},{17,25},{2,10},{10,18},{18,26},{... | collective-permute-start | bytes 36872 | tf_op jit(solution)/shard_map/ppermute | solution.py:14
  75.7 1.3 collective-permute-start.16
  77.0 2.4 %collective-permute-done.16 = f32[3,1,8,128]{3,2,1,0:T(8,128)S(1)} collective-permute-done((f32[3,1,8,128]{3,2,1,0:T(8,128)S(1)}, f32[3,1,8,128]{3,2,1,0:T(8,128)S(1)}, u32[]{:S(2)}, u32[]{:S(2)}) %collective-permute-start.16) | collective-permute-done | bytes 12320 | tf_op jit(solution)/shard_map/ppermute | solution.py:15
  79.5 4.8 %collective-permute-start.19 = (f32[3,10,1,128]{3,2,1,0:T(1,128)S(1)}, f32[3,10,1,128]{3,2,1,0:T(1,128)S(1)}, u32[]{:S(2)}, u32[]{:S(2)}) collective-permute-start(f32[3,10,1,128]{3,2,1,0:T(1,128)S(1)} %get-tuple-element.11), channel_id=1, source_target_pairs={{0,1},{1,2},{2,3},{3,4},{4,5},{5,6},{6,7},{8,9},{9,10},{10,11},{11... | collective-permute-start | bytes 46088 | tf_op jit(solution)/shard_map/ppermute | solution.py:14
  84.3 1.3 collective-permute-start.18
  85.6 1.0 pad.195
  86.6 6.3 %copy.21 = f32[8,8,192,128]{3,1,2,0:T(8,128)} copy(f32[8,8,192,128]{3,2,1,0:T(8,128)S(1)} %bitcast.40) | data formatting | bytes 12582912
  93.2 1.0 fusion.7
  94.3 17.7 %concatenate.123 = f32[64,24576]{1,0:T(8,128)} concatenate(f32[60,24576]{1,0:T(8,128)} %bitcast.38, f32[1,24576]{1,0:T(1,128)S(1)} %bitcast.42, f32[1,24576]{1,0:T(1,128)S(1)} %bitcast.43, f32[1,24576]{1,0:T(1,128)S(1)} %bitcast.44, f32[1,24576]{1,0:T(1,128)S(1)} %bitcast.45), dimensions={0} | concatenate | bytes 12582912 | tf_op jit(solution)/shard_map/concatenate | solution.py:72
  112.0 8.2 %convolution_multiply_fusion = f32[64,64]{0,1:T(8,128)S(1)} fusion(f32[64,24576]{1,0:T(8,128)} %concatenate.123), kind=kOutput, calls=%fused_computation.2 | convolution fusion | flops 1207963648 | bytes 6307840 | tf_op jit(solution)/shard_map/dot_general | solution.py:39
  120.2 12.3 %psum.14 = f32[64,64]{0,1:T(8,128)S(1)} all-reduce(f32[64,64]{0,1:T(8,128)S(1)} %convolution_multiply_fusion), channel_id=1, replica_groups=mesh['gx'=4,'gy'=8] {'gx'}, use_global_device_ids=true, to_apply=%region_0.1 | all-reduce | flops 4096 | bytes 32768 | tf_op jit(solution)/shard_map/psum | solution.py:48
  132.5 35.4 %psum.15 = f32[64,64]{0,1:T(8,128)S(1)} all-reduce(f32[64,64]{0,1:T(8,128)S(1)} %psum.14), channel_id=1, replica_groups=mesh['gx'=4,'gy'=8] {'gy'}, use_global_device_ids=true, to_apply=%region_1.2 | all-reduce | flops 4096 | bytes 32768 | tf_op jit(solution)/shard_map/psum | solution.py:48
  168.0 5.8 %cholesky.16 = f32[64,64]{1,0:T(8,128)S(1)} custom-call(f32[64,64]{1,0:T(8,128)S(1)} %fusion.83), custom_call_target="Cholesky" | custom-call | tf_op jit(solution)/shard_map/jit(cholesky)/cholesky | solution.py:48
  175.2 0.7 copy.17
  175.9 4.9 %custom-call.7 = f32[1,64,64]{1,2,0:T(8,128)S(1)} custom-call(f32[1,64,64]{2,1,0:T(8,128)S(1)} %get-tuple-element.32), custom_call_target="InvertDiagBlocksLowerTriangular" | custom-call | tf_op jit(solution)/shard_map/jit(_solve_triangular)/triangular_solve | solution.py:49
  180.8 3.9 %copy.22 = f32[8,8,192,128]{3,2,1,0:T(8,128)S(1)} copy(f32[8,8,192,128]{3,1,2,0:T(8,128)} %bitcast.37) | data formatting | bytes 12582912
  184.7 9.3 %fusion = f32[64,3,8,8,128]{4,0,3,2,1:T(8,128)S(1)} fusion(f32[3,8,8,128,64]{3,2,1,0,4:T(8,128)S(1)} %bitcast.39, f32[1,64,64]{1,2,0:T(8,128)S(1)} %custom-call.7), kind=kOutput, calls=%fused_computation | convolution fusion | flops 1207959552 | bytes 12599296 | tf_op jit(solution)/shard_map/jit(_solve_triangular)/triangular_solve | solution.py:49
  194.1 6.6 %copy.16 = f32[64,3,8,8,128]{4,3,2,1,0:T(8,128)} copy(f32[64,3,8,8,128]{4,0,3,2,1:T(8,128)S(1)} %fusion) | data formatting | bytes 12582912
  (39 shorter events, 3.9 us)
Async XLA Ops:
  0.6 85.0 %copy-start = (f32[60,3,8,8,128]{4,3,2,1,0:T(8,128)S(1)}, f32[60,3,8,8,128]{4,3,2,1,0:T(8,128)}, u32[]{:S(2)}) copy-start(f32[60,3,8,8,128]{4,3,2,1,0:T(8,128)} %param.7) | copy-start | bytes 17694724
  1.5 3.9 %collective-permute-start.2 = (f32[1,8,128]{2,1,0:T(8,128)S(1)}, f32[1,8,128]{2,1,0:T(8,128)S(1)}, u32[]{:S(2)}, u32[]{:S(2)}) collective-permute-start(f32[1,8,128]{2,1,0:T(8,128)S(1)} %get-tuple-element.39), channel_id=1, source_target_pairs={{0,8},{8,16},{16,24},{1,9},{9,17},{17,25},{2,10},{10,18},{18,26},{... | collective-permute-start | bytes 12296 | tf_op jit(solution)/shard_map/ppermute | solution.py:14
  4.1 5.2 %collective-permute-start = (f32[1,8,128]{2,1,0:T(8,128)S(1)}, f32[1,8,128]{2,1,0:T(8,128)S(1)}, u32[]{:S(2)}, u32[]{:S(2)}) collective-permute-start(f32[1,8,128]{2,1,0:T(8,128)S(1)} %get-tuple-element.38), channel_id=1, source_target_pairs={{8,0},{16,8},{24,16},{9,1},{17,9},{25,17},{10,2},{18,10},{26,18},{... | collective-permute-start | bytes 12296 | tf_op jit(solution)/shard_map/ppermute | solution.py:15
  10.2 11.3 %collective-permute-start.6 = (f32[10,1,128]{2,1,0:T(1,128)S(1)}, f32[10,1,128]{2,1,0:T(1,128)S(1)}, u32[]{:S(2)}, u32[]{:S(2)}) collective-permute-start(f32[10,1,128]{2,1,0:T(1,128)S(1)} %get-tuple-element.29), channel_id=1, source_target_pairs={{0,1},{1,2},{2,3},{3,4},{4,5},{5,6},{6,7},{8,9},{9,10},{10,11},{11... | collective-permute-start | bytes 15368 | tf_op jit(solution)/shard_map/ppermute | solution.py:14
  13.6 8.0 %collective-permute-start.4 = (f32[10,1,128]{2,1,0:T(1,128)S(1)}, f32[10,1,128]{2,1,0:T(1,128)S(1)}, u32[]{:S(2)}, u32[]{:S(2)}) collective-permute-start(f32[10,1,128]{2,1,0:T(1,128)S(1)} %get-tuple-element.30), channel_id=1, source_target_pairs={{1,0},{2,1},{3,2},{4,3},{5,4},{6,5},{7,6},{9,8},{10,9},{11,10},{12... | collective-permute-start | bytes 15368 | tf_op jit(solution)/shard_map/ppermute | solution.py:15
  15.6 7.6 %collective-permute-start.1 = (f32[3,1,8,128]{3,2,1,0:T(8,128)S(1)}, f32[3,1,8,128]{3,2,1,0:T(8,128)S(1)}, u32[]{:S(2)}, u32[]{:S(2)}) collective-permute-start(f32[3,1,8,128]{3,2,1,0:T(8,128)S(1)} %get-tuple-element.25), channel_id=1, source_target_pairs={{8,0},{16,8},{24,16},{9,1},{17,9},{25,17},{10,2},{18,10},{26,18},{... | collective-permute-start | bytes 36872 | tf_op jit(solution)/shard_map/ppermute | solution.py:15
  16.9 5.4 %collective-permute-start.3 = (f32[3,1,8,128]{3,2,1,0:T(8,128)S(1)}, f32[3,1,8,128]{3,2,1,0:T(8,128)S(1)}, u32[]{:S(2)}, u32[]{:S(2)}) collective-permute-start(f32[3,1,8,128]{3,2,1,0:T(8,128)S(1)} %get-tuple-element.26), channel_id=1, source_target_pairs={{0,8},{8,16},{16,24},{1,9},{9,17},{17,25},{2,10},{10,18},{18,26},{... | collective-permute-start | bytes 36872 | tf_op jit(solution)/shard_map/ppermute | solution.py:14
  23.3 6.4 %collective-permute-start.7 = (f32[3,10,1,128]{3,2,1,0:T(1,128)S(1)}, f32[3,10,1,128]{3,2,1,0:T(1,128)S(1)}, u32[]{:S(2)}, u32[]{:S(2)}) collective-permute-start(f32[3,10,1,128]{3,2,1,0:T(1,128)S(1)} %get-tuple-element.17), channel_id=1, source_target_pairs={{0,1},{1,2},{2,3},{3,4},{4,5},{5,6},{6,7},{8,9},{9,10},{10,11},{11... | collective-permute-start | bytes 46088 | tf_op jit(solution)/shard_map/ppermute | solution.py:14
  27.6 6.1 %collective-permute-start.5 = (f32[3,10,1,128]{3,2,1,0:T(1,128)S(1)}, f32[3,10,1,128]{3,2,1,0:T(1,128)S(1)}, u32[]{:S(2)}, u32[]{:S(2)}) collective-permute-start(f32[3,10,1,128]{3,2,1,0:T(1,128)S(1)} %get-tuple-element.18), channel_id=1, source_target_pairs={{1,0},{2,1},{3,2},{4,3},{5,4},{6,5},{7,6},{9,8},{10,9},{11,10},{12... | collective-permute-start | bytes 46088 | tf_op jit(solution)/shard_map/ppermute | solution.py:15
  35.2 3.8 %collective-permute-start.9 = (f32[3,1,8,128]{3,2,1,0:T(8,128)S(1)}, f32[3,1,8,128]{3,2,1,0:T(8,128)S(1)}, u32[]{:S(2)}, u32[]{:S(2)}) collective-permute-start(f32[3,1,8,128]{3,2,1,0:T(8,128)S(1)} %get-tuple-element.23), channel_id=1, source_target_pairs={{0,8},{8,16},{16,24},{1,9},{9,17},{17,25},{2,10},{10,18},{18,26},{... | collective-permute-start | bytes 36872 | tf_op jit(solution)/shard_map/ppermute | solution.py:14
  37.7 6.0 %collective-permute-start.8 = (f32[3,1,8,128]{3,2,1,0:T(8,128)S(1)}, f32[3,1,8,128]{3,2,1,0:T(8,128)S(1)}, u32[]{:S(2)}, u32[]{:S(2)}) collective-permute-start(f32[3,1,8,128]{3,2,1,0:T(8,128)S(1)} %get-tuple-element.24), channel_id=1, source_target_pairs={{8,0},{16,8},{24,16},{9,1},{17,9},{25,17},{10,2},{18,10},{26,18},{... | collective-permute-start | bytes 36872 | tf_op jit(solution)/shard_map/ppermute | solution.py:15
  43.7 6.2 %collective-permute-start.11 = (f32[3,10,1,128]{3,2,1,0:T(1,128)S(1)}, f32[3,10,1,128]{3,2,1,0:T(1,128)S(1)}, u32[]{:S(2)}, u32[]{:S(2)}) collective-permute-start(f32[3,10,1,128]{3,2,1,0:T(1,128)S(1)} %get-tuple-element.15), channel_id=1, source_target_pairs={{0,1},{1,2},{2,3},{3,4},{4,5},{5,6},{6,7},{8,9},{9,10},{10,11},{11... | collective-permute-start | bytes 46088 | tf_op jit(solution)/shard_map/ppermute | solution.py:14
  48.6 5.6 %collective-permute-start.10 = (f32[3,10,1,128]{3,2,1,0:T(1,128)S(1)}, f32[3,10,1,128]{3,2,1,0:T(1,128)S(1)}, u32[]{:S(2)}, u32[]{:S(2)}) collective-permute-start(f32[3,10,1,128]{3,2,1,0:T(1,128)S(1)} %get-tuple-element.16), channel_id=1, source_target_pairs={{1,0},{2,1},{3,2},{4,3},{5,4},{6,5},{7,6},{9,8},{10,9},{11,10},{12... | collective-permute-start | bytes 46088 | tf_op jit(solution)/shard_map/ppermute | solution.py:15
  55.6 4.2 %collective-permute-start.13 = (f32[3,1,8,128]{3,2,1,0:T(8,128)S(1)}, f32[3,1,8,128]{3,2,1,0:T(8,128)S(1)}, u32[]{:S(2)}, u32[]{:S(2)}) collective-permute-start(f32[3,1,8,128]{3,2,1,0:T(8,128)S(1)} %get-tuple-element.21), channel_id=1, source_target_pairs={{0,8},{8,16},{16,24},{1,9},{9,17},{17,25},{2,10},{10,18},{18,26},{... | collective-permute-start | bytes 36872 | tf_op jit(solution)/shard_map/ppermute | solution.py:14
  58.5 4.0 %collective-permute-start.12 = (f32[3,1,8,128]{3,2,1,0:T(8,128)S(1)}, f32[3,1,8,128]{3,2,1,0:T(8,128)S(1)}, u32[]{:S(2)}, u32[]{:S(2)}) collective-permute-start(f32[3,1,8,128]{3,2,1,0:T(8,128)S(1)} %get-tuple-element.22), channel_id=1, source_target_pairs={{8,0},{16,8},{24,16},{9,1},{17,9},{25,17},{10,2},{18,10},{26,18},{... | collective-permute-start | bytes 36872 | tf_op jit(solution)/shard_map/ppermute | solution.py:15
  62.5 4.4 %collective-permute-start.15 = (f32[3,10,1,128]{3,2,1,0:T(1,128)S(1)}, f32[3,10,1,128]{3,2,1,0:T(1,128)S(1)}, u32[]{:S(2)}, u32[]{:S(2)}) collective-permute-start(f32[3,10,1,128]{3,2,1,0:T(1,128)S(1)} %get-tuple-element.13), channel_id=1, source_target_pairs={{0,1},{1,2},{2,3},{3,4},{4,5},{5,6},{6,7},{8,9},{9,10},{10,11},{11... | collective-permute-start | bytes 46088 | tf_op jit(solution)/shard_map/ppermute | solution.py:14
  65.5 5.6 %collective-permute-start.14 = (f32[3,10,1,128]{3,2,1,0:T(1,128)S(1)}, f32[3,10,1,128]{3,2,1,0:T(1,128)S(1)}, u32[]{:S(2)}, u32[]{:S(2)}) collective-permute-start(f32[3,10,1,128]{3,2,1,0:T(1,128)S(1)} %get-tuple-element.14), channel_id=1, source_target_pairs={{1,0},{2,1},{3,2},{4,3},{5,4},{6,5},{7,6},{9,8},{10,9},{11,10},{12... | collective-permute-start | bytes 46088 | tf_op jit(solution)/shard_map/ppermute | solution.py:15
  72.5 4.5 %collective-permute-start.17 = (f32[3,1,8,128]{3,2,1,0:T(8,128)S(1)}, f32[3,1,8,128]{3,2,1,0:T(8,128)S(1)}, u32[]{:S(2)}, u32[]{:S(2)}) collective-permute-start(f32[3,1,8,128]{3,2,1,0:T(8,128)S(1)} %get-tuple-element.19), channel_id=1, source_target_pairs={{0,8},{8,16},{16,24},{1,9},{9,17},{17,25},{2,10},{10,18},{18,26},{... | collective-permute-start | bytes 36872 | tf_op jit(solution)/shard_map/ppermute | solution.py:14
  75.7 3.8 %collective-permute-start.16 = (f32[3,1,8,128]{3,2,1,0:T(8,128)S(1)}, f32[3,1,8,128]{3,2,1,0:T(8,128)S(1)}, u32[]{:S(2)}, u32[]{:S(2)}) collective-permute-start(f32[3,1,8,128]{3,2,1,0:T(8,128)S(1)} %get-tuple-element.20), channel_id=1, source_target_pairs={{8,0},{16,8},{24,16},{9,1},{17,9},{25,17},{10,2},{18,10},{26,18},{... | collective-permute-start | bytes 36872 | tf_op jit(solution)/shard_map/ppermute | solution.py:15
  79.5 13.4 %collective-permute-start.19 = (f32[3,10,1,128]{3,2,1,0:T(1,128)S(1)}, f32[3,10,1,128]{3,2,1,0:T(1,128)S(1)}, u32[]{:S(2)}, u32[]{:S(2)}) collective-permute-start(f32[3,10,1,128]{3,2,1,0:T(1,128)S(1)} %get-tuple-element.11), channel_id=1, source_target_pairs={{0,1},{1,2},{2,3},{3,4},{4,5},{5,6},{6,7},{8,9},{9,10},{10,11},{11... | collective-permute-start | bytes 46088 | tf_op jit(solution)/shard_map/ppermute | solution.py:14
  84.3 8.6 %collective-permute-start.18 = (f32[3,10,1,128]{3,2,1,0:T(1,128)S(1)}, f32[3,10,1,128]{3,2,1,0:T(1,128)S(1)}, u32[]{:S(2)}, u32[]{:S(2)}) collective-permute-start(f32[3,10,1,128]{3,2,1,0:T(1,128)S(1)} %get-tuple-element.12), channel_id=1, source_target_pairs={{1,0},{2,1},{3,2},{4,3},{5,4},{6,5},{7,6},{9,8},{10,9},{11,10},{12... | collective-permute-start | bytes 46088 | tf_op jit(solution)/shard_map/ppermute | solution.py:15
  94.3 17.7 %copy-start.1 = (f32[3,8,8,128]{3,2,1,0:T(8,128)}, f32[3,8,8,128]{3,2,1,0:T(8,128)S(1)}, u32[]{:S(2)}) copy-start(f32[3,8,8,128]{3,2,1,0:T(8,128)S(1)} %fusion.7) | copy-start | bytes 294916
